TPU v7x, 512 devices: a whole 4x4x16 slice. The times are simulated.
512 devices in a mesh: expert: 128 (over y, x_lo, z), half: 4 (over x_hi, core).
Axes of the slice: x: 4 (x_hi: 2, x_lo: 2; x = x_hi * 2 + x_lo), y: 4, z: 16, core: 2. Of those that a mesh axis runs over, the one named last changes fastest.
Arguments:
- tokens: bfloat16 [25088, 1024], P('expert', 'half'), may hold values from -128 to 128
- slot_params: bfloat16 [1024, 256], P('half'), may hold values from -0.5 to 0.5
- w_up: bfloat16 [128, 1024, 4096], P('expert', None, 'half'), may hold values from -0.1875 to 0.1875
- w_down: bfloat16 [128, 4096, 1024], P('expert', 'half'), may hold values from -0.09375 to 0.09375
- cotangent: bfloat16 [25088, 1024], P('expert', 'half'), may hold values from -6 to 6
Outputs:
- mixed: bfloat16 [25088, 1024], P('expert', 'half')
- grad_tokens: bfloat16 [25088, 1024], P('expert', 'half')
- grad_params: float32 [1024, 256], P('half')
All inputs are finite; a program needn't handle non-finite values.
Results may differ from a plain program's by a relative error of at most 0.017.
Values may be sent and summed in bfloat16 or wider, within the bound.
A program may use at most 64 MiB of HBM per device.

v0:
```python
import jax
import jax.numpy as jnp
from jax import lax
from jax.sharding import PartitionSpec as P

SEQ = 196
SLOTS = 2
EXPERT = ("y", "x_lo", "z")
HALF = ("x_hi", "core")


def gelu_grad(preact, upstream):
    pullback = jax.vjp(jax.nn.gelu, preact)[1]
    return pullback(upstream)[0]


def softmax_back(probabilities, upstream, over_axis):
    inner = jnp.sum(probabilities * upstream, axis=over_axis, keepdims=True)
    return probabilities * (upstream - inner)


def local(tokens, slot_params, w_up, w_down, cotangent):
    feat_quarter = tokens.shape[1]
    images = tokens.shape[0] // SEQ
    columns = slot_params.shape[1]
    experts = columns // SLOTS
    up_matrix = w_up[0]
    down_matrix = w_down[0]
    inputs = tokens.reshape(images, SEQ, feat_quarter)
    upstream = cotangent.reshape(images, SEQ, feat_quarter)
    partial_logits = jnp.einsum(
        "imf,fc->imc", inputs, slot_params, preferred_element_type=jnp.float32
    )
    logits = lax.psum(partial_logits, HALF)
    dispatch = jax.nn.softmax(logits, axis=1)
    combine = jax.nn.softmax(logits, axis=2)
    dispatch_bf = dispatch.astype(jnp.bfloat16).reshape(images, SEQ, experts, SLOTS)
    combine_bf = combine.astype(jnp.bfloat16).reshape(images, SEQ, experts, SLOTS)
    slot_in = jnp.einsum(
        "imes,imf->sife", dispatch_bf, inputs, preferred_element_type=jnp.float32
    ).astype(jnp.bfloat16)
    received = lax.all_to_all(slot_in, EXPERT, split_axis=3, concat_axis=3, tiled=True)
    up_slice = up_matrix
    preact = jnp.einsum(
        "sifr,fk->sirk",
        lax.all_gather(received, HALF, axis=2, tiled=True),
        up_slice,
        preferred_element_type=jnp.float32,
    )
    hidden = jax.nn.gelu(preact).astype(jnp.bfloat16)
    down_slice = down_matrix
    summed = lax.psum(
        jnp.einsum("kf,sirk->fsir", down_slice, hidden, preferred_element_type=jnp.float32).astype(
            jnp.bfloat16
        ),
        HALF,
    ).astype(jnp.float32)
    slot_out = lax.dynamic_slice_in_dim(
        summed, lax.axis_index(HALF) * feat_quarter, feat_quarter, 0
    )
    returned = lax.all_to_all(
        slot_out.astype(jnp.bfloat16), EXPERT, split_axis=3, concat_axis=3, tiled=True
    )
    mixed = jnp.einsum(
        "imes,fsie->imf", combine_bf, returned, preferred_element_type=jnp.float32
    ).astype(jnp.bfloat16)
    grad_slot_out = jnp.einsum(
        "imes,imf->sife", combine_bf, upstream, preferred_element_type=jnp.float32
    ).astype(jnp.bfloat16)
    combine_part = jnp.einsum(
        "imf,fsie->imes", upstream, returned, preferred_element_type=jnp.float32
    ).reshape(images, SEQ, columns)
    grad_combine = lax.psum(combine_part.astype(jnp.bfloat16), HALF).astype(jnp.float32)
    grad_received = lax.all_to_all(grad_slot_out, EXPERT, split_axis=3, concat_axis=3, tiled=True)
    down_slice = down_matrix
    grad_hidden = jnp.einsum(
        "sifr,kf->sirk",
        lax.all_gather(grad_received, HALF, axis=2, tiled=True),
        down_slice,
        preferred_element_type=jnp.float32,
    )
    grad_preact = gelu_grad(preact, grad_hidden).astype(jnp.bfloat16)
    up_slice = up_matrix
    summed_grad = lax.psum(
        jnp.einsum(
            "fk,sirk->fsir", up_slice, grad_preact, preferred_element_type=jnp.float32
        ).astype(jnp.bfloat16),
        HALF,
    ).astype(jnp.float32)
    grad_slot_in = lax.dynamic_slice_in_dim(
        summed_grad, lax.axis_index(HALF) * feat_quarter, feat_quarter, 0
    )
    grad_returned = lax.all_to_all(
        grad_slot_in.astype(jnp.bfloat16), EXPERT, split_axis=3, concat_axis=3, tiled=True
    )
    dispatch_part = jnp.einsum(
        "imf,fsie->imes", inputs, grad_returned, preferred_element_type=jnp.float32
    ).reshape(images, SEQ, columns)
    grad_dispatch = lax.psum(dispatch_part.astype(jnp.bfloat16), HALF).astype(jnp.float32)
    grad_logits = softmax_back(combine, grad_combine, 2) + softmax_back(dispatch, grad_dispatch, 1)
    grad_logit_bf = grad_logits.astype(jnp.bfloat16)
    token_term = jnp.einsum(
        "imes,fsie->imf", dispatch_bf, grad_returned, preferred_element_type=jnp.float32
    )
    logit_term = jnp.einsum(
        "imc,fc->imf", grad_logit_bf, slot_params, preferred_element_type=jnp.float32
    )
    grad_tokens = (token_term + logit_term).astype(jnp.bfloat16).reshape(images * SEQ, feat_quarter)
    params_part = jnp.einsum(
        "imf,imc->fc", inputs, grad_logit_bf, preferred_element_type=jnp.float32
    )
    grad_params = lax.psum(lax.psum(lax.psum(params_part, "z"), "y"), "x_lo")
    return (mixed.reshape(images * SEQ, feat_quarter), grad_tokens, grad_params)


def solution(mesh):
    mesh = jax.sharding.Mesh(mesh.devices.reshape(4, 2, 16, 2, 2), EXPERT + HALF)
    in_specs = (
        P(EXPERT, HALF),
        P(HALF, None),
        P(EXPERT, None, HALF),
        P(EXPERT, HALF, None),
        P(EXPERT, HALF),
    )
    out_specs = (P(EXPERT, HALF), P(EXPERT, HALF), P(HALF, None))
    return jax.shard_map(local, mesh=mesh, in_specs=in_specs, out_specs=out_specs, check_vma=False)
```

profile of v0, /device:TPU:1, one launch (start us, length us, event | category | flops | bytes accessed | tf_op | source)
XLA Modules:
  0.0 566.3 jit_solution(11431547479652277655)
XLA Ops:
  7.2 2.0 convolution_bitcast_fusion.3
  9.2 64.2 %all-reduce.9.cloned.1.call-done = f32[1,196,256]{2,1,0:T(8,128)} async-done(((f32[1,196,256]{2,1,0:T(8,128)}), f32[1,196,256]{2,1,0:T(8,128)}) %all-reduce.9.cloned.1.call-update) | async-done | bytes 200720 | tf_op jit(solution)/shard_map/psum | solution.py:34
  73.4 1.0 fusion.82
  74.5 1.1 fusion.60
  75.6 1.1 fusion.80
  78.1 16.6 %all-to-all-start = ((bf16[2,1,256,128]{2,0,1,3:T(2,128)(2,1)}), bf16[2,1,256,128]{2,0,1,3:T(2,128)(2,1)S(1)}, u32[]{:S(2)}, u32[]{:S(2)}) async-start(bf16[2,1,256,128]{2,0,1,3:T(2,128)(2,1)} %copy.37), calls=%async_computation | async-start | bytes 262144 | tf_op jit(solution)/shard_map/all_to_all | solution.py:42
  96.1 15.3 %all-to-all-done = bf16[2,1,256,128]{2,0,1,3:T(2,128)(2,1)S(1)} async-done(((bf16[2,1,256,128]{2,0,1,3:T(2,128)(2,1)}), bf16[2,1,256,128]{2,0,1,3:T(2,128)(2,1)S(1)}, u32[]{:S(2)}, u32[]{:S(2)}) %all-to-all-start) | async-done | bytes 131104 | tf_op jit(solution)/shard_map/all_to_all | solution.py:42
  111.4 6.6 %all-to-all-start.2 = ((bf16[2,1,256,128]{2,0,1,3:T(2,128)(2,1)}), bf16[2,1,256,128]{2,0,1,3:T(2,128)(2,1)S(1)}, u32[]{:S(2)}, u32[]{:S(2)}) async-start(bf16[2,1,256,128]{2,0,1,3:T(2,128)(2,1)} %copy.43), calls=%async_computation.2 | async-start | bytes 262144 | tf_op jit(solution)/shard_map/all_to_all | solution.py:74
  118.1 10.0 %all_gather.6 = bf16[2,1,1024,128]{2,3,0,1:T(8,128)(2,1)S(1)} all-gather(bf16[2,1,256,128]{2,3,0,1:T(8,128)(2,1)S(1)} %copy.38), channel_id=1, replica_groups=mesh['y'=4,'x_lo'=2,'z'=16,'x_hi'=2,'core'=2] {'x_hi','core'}, dimensions={2}, use_global_device_ids=true | all-gather | bytes 655360 | tf_op jit(solution)/shard_map/all_gather | solution.py:46
  128.1 5.5 all-to-all-done.2
  133.6 11.5 %all_gather.7 = bf16[2,1,1024,128]{2,3,0,1:T(8,128)(2,1)S(1)} all-gather(bf16[2,1,256,128]{2,3,0,1:T(8,128)(2,1)S(1)} %copy.44), channel_id=1, replica_groups=mesh['y'=4,'x_lo'=2,'z'=16,'x_hi'=2,'core'=2] {'x_hi','core'}, dimensions={2}, use_global_device_ids=true | all-gather | bytes 655360 | tf_op jit(solution)/shard_map/all_gather | solution.py:78
  145.1 2.3 fusion.6
  147.4 1.0 copy-done.3
  148.4 1.6 fusion.14
  150.0 4.5 fusion.17
  154.5 52.4 %all-reduce.19.cloned.1.call-done = (bf16[1024,2,1,128]{0,3,1,2:T(8,128)(2,1)}, bf16[1024,2,1,128]{0,3,1,2:T(8,128)(2,1)}) async-done(((bf16[1024,2,1,128]{0,3,1,2:T(8,128)(2,1)}, bf16[1024,2,1,128]{0,3,1,2:T(8,128)(2,1)}), (bf16[1024,2,1,128]{0,3,1,2:T(8,128)(2,1)}, bf16[1024,2,1,128]{0,3,1,2:T(8,128)(2,1)})) %all-reduce.19.cloned.1.call-update) | async-done | bytes 1048592 | tf_op jit(solution)/shard_map/psum | solution.py:52
  207.0 0.9 convert_convert_fusion
  208.7 16.6 %all-to-all-start.3 = ((bf16[256,2,1,128]{0,1,2,3:T(2,128)(2,1)}), bf16[256,2,1,128]{0,1,2,3:T(2,128)(2,1)S(1)}, u32[]{:S(2)}, u32[]{:S(2)}) async-start(bf16[256,2,1,128]{0,1,2,3:T(2,128)(2,1)} %copy.45), calls=%async_computation.3 | async-start | bytes 262144 | tf_op jit(solution)/shard_map/all_to_all | solution.py:93
  225.3 0.9 convert_convert_fusion.1
  227.0 15.0 %all-to-all-done.3 = bf16[256,2,1,128]{0,1,2,3:T(2,128)(2,1)S(1)} async-done(((bf16[256,2,1,128]{0,1,2,3:T(2,128)(2,1)}), bf16[256,2,1,128]{0,1,2,3:T(2,128)(2,1)S(1)}, u32[]{:S(2)}, u32[]{:S(2)}) %all-to-all-start.3) | async-done | bytes 131104 | tf_op jit(solution)/shard_map/all_to_all | solution.py:93
  242.0 6.8 %all-to-all-start.1 = ((bf16[256,2,1,128]{0,1,2,3:T(2,128)(2,1)}), bf16[256,2,1,128]{0,1,2,3:T(2,128)(2,1)S(1)}, u32[]{:S(2)}, u32[]{:S(2)}) async-start(bf16[256,2,1,128]{0,1,2,3:T(2,128)(2,1)} %copy.39), calls=%async_computation.1 | async-start | bytes 262144 | tf_op jit(solution)/shard_map/all_to_all | solution.py:61
  250.3 14.1 %all-to-all-done.1 = bf16[256,2,1,128]{0,1,2,3:T(2,128)(2,1)S(1)} async-done(((bf16[256,2,1,128]{0,1,2,3:T(2,128)(2,1)}), bf16[256,2,1,128]{0,1,2,3:T(2,128)(2,1)S(1)}, u32[]{:S(2)}, u32[]{:S(2)}) %all-to-all-start.1) | async-done | bytes 131104 | tf_op jit(solution)/shard_map/all_to_all | solution.py:61
  265.8 48.2 %all-reduce.17.cloned.1.call-done = (bf16[1,196,256]{2,1,0:T(8,128)(2,1)}, bf16[1,196,256]{2,1,0:T(8,128)(2,1)}) async-done(((bf16[1,196,256]{2,1,0:T(8,128)(2,1)}, bf16[1,196,256]{2,1,0:T(8,128)(2,1)}), (bf16[1,196,256]{2,1,0:T(8,128)(2,1)}, bf16[1,196,256]{2,1,0:T(8,128)(2,1)})) %all-reduce.17.cloned.1.call-update) | async-done | bytes 200720 | tf_op jit(solution)/shard_map/psum | solution.py:99
  314.0 1.2 fusion.51
  315.2 1.1 fusion.65
  316.3 0.9 convolution_bitcast_fusion
  317.3 126.5 %all-reduce.11.cloned.1.call-done = f32[256,256]{0,1:T(8,128)} async-done(((f32[256,256]{0,1:T(8,128)}), f32[256,256]{0,1:T(8,128)}) %all-reduce.11.cloned.1.call-update) | async-done | bytes 262160 | tf_op jit(solution)/shard_map/psum | solution.py:112
  443.9 0.9 fusion.20
  444.8 62.7 %all-reduce.13.cloned.1.call-done = f32[256,256]{0,1:T(8,128)} async-done(((f32[256,256]{0,1:T(8,128)}), f32[256,256]{0,1:T(8,128)}) %all-reduce.13.cloned.1.call-update) | async-done | bytes 262160 | tf_op jit(solution)/shard_map/psum | solution.py:112
  507.7 0.9 fusion.21
  508.6 49.1 %all-reduce.15.cloned.1.call-done = f32[256,256]{0,1:T(8,128)} async-done(((f32[256,256]{0,1:T(8,128)}), f32[256,256]{0,1:T(8,128)}) %all-reduce.15.cloned.1.call-update) | async-done | bytes 262160 | tf_op jit(solution)/shard_map/psum | solution.py:112
  557.6 1.8 copy.52
  (66 shorter events, 7.6 us)
Async XLA Ops:
  7.2 141.2 %copy-start = (bf16[1,1024,1024]{2,1,0:T(8,128)(2,1)S(1)}, bf16[1,1024,1024]{2,1,0:T(8,128)(2,1)}, u32[]{:S(2)}) copy-start(bf16[1,1024,1024]{2,1,0:T(8,128)(2,1)} %param.8) | copy-start | bytes 6291460
  7.2 69.9 %copy-start.2 = (bf16[196,256]{1,0:T(8,128)(2,1)S(1)}, bf16[196,256]{1,0:T(8,128)(2,1)}, u32[]{:S(2)}) copy-start(bf16[196,256]{1,0:T(8,128)(2,1)} %param.5) | copy-start | bytes 301060
  7.2 87.9 %copy-start.5 = (bf16[196,256]{1,0:T(8,128)(2,1)S(1)}, bf16[196,256]{1,0:T(8,128)(2,1)}, u32[]{:S(2)}) copy-start(bf16[196,256]{1,0:T(8,128)(2,1)} %param.9) | copy-start | bytes 301060
  7.2 66.2 %all-reduce.9.cloned.1.call-start = ((), (), s32[]{:S(2)}) async-start(), calls=%async_computation.4 | async-start | bytes 409600 | tf_op jit(solution)/shard_map/psum | solution.py:34
  74.5 2.2 copy-start.7
  74.5 2.2 copy-start.9
  75.6 1.1 copy-start.11
  75.6 1.1 copy-start.13
  78.1 33.3 %all-to-all-start = ((bf16[2,1,256,128]{2,0,1,3:T(2,128)(2,1)}), bf16[2,1,256,128]{2,0,1,3:T(2,128)(2,1)S(1)}, u32[]{:S(2)}, u32[]{:S(2)}) async-start(bf16[2,1,256,128]{2,0,1,3:T(2,128)(2,1)} %copy.37), calls=%async_computation | async-start | bytes 262144 | tf_op jit(solution)/shard_map/all_to_all | solution.py:42
  111.4 22.2 %all-to-all-start.2 = ((bf16[2,1,256,128]{2,0,1,3:T(2,128)(2,1)}), bf16[2,1,256,128]{2,0,1,3:T(2,128)(2,1)S(1)}, u32[]{:S(2)}, u32[]{:S(2)}) async-start(bf16[2,1,256,128]{2,0,1,3:T(2,128)(2,1)} %copy.43), calls=%async_computation.2 | async-start | bytes 262144 | tf_op jit(solution)/shard_map/all_to_all | solution.py:74
  118.1 88.9 %all-reduce.19.cloned.1.call-start = ((), (), s32[]{:S(2)}) async-start(), calls=%async_computation.9 | async-start | bytes 2097152 | tf_op jit(solution)/shard_map/psum | solution.py:52
  147.4 1.0 copy-start.3
  154.5 110.0 %copy-start.6 = (bf16[196,256]{1,0:T(8,128)(2,1)S(1)}, bf16[196,256]{1,0:T(8,128)(2,1)}, u32[]{:S(2)}) copy-start(bf16[196,256]{1,0:T(8,128)(2,1)} %param.9) | copy-start | bytes 301060
  207.9 106.2 %copy-start.1 = (f32[1,196,256]{2,1,0:T(8,128)S(1)}, f32[1,196,256]{2,1,0:T(8,128)}, u32[]{:S(2)}) copy-start(f32[1,196,256]{2,1,0:T(8,128)} %all-reduce.9.cloned.1.call-done) | copy-start | bytes 602116
  207.9 106.1 %copy-start.8 = (f32[256]{0:T(256)S(1)}, f32[256]{0:T(256)}, u32[]{:S(2)}) copy-start(f32[256]{0:T(256)} %copy-done.7) | copy-start | bytes 3076
  207.9 106.1 %copy-start.10 = (f32[196]{0:T(256)S(1)}, f32[196]{0:T(256)}, u32[]{:S(2)}) copy-start(f32[196]{0:T(256)} %copy-done.9) | copy-start | bytes 2356
  207.9 106.1 %copy-start.12 = (f32[256]{0:T(256)S(1)}, f32[256]{0:T(256)}, u32[]{:S(2)}) copy-start(f32[256]{0:T(256)} %copy-done.11) | copy-start | bytes 3076
  207.9 106.1 %copy-start.14 = (f32[196]{0:T(256)S(1)}, f32[196]{0:T(256)}, u32[]{:S(2)}) copy-start(f32[196]{0:T(256)} %copy-done.13) | copy-start | bytes 2356
  208.7 33.3 %all-to-all-start.3 = ((bf16[256,2,1,128]{0,1,2,3:T(2,128)(2,1)}), bf16[256,2,1,128]{0,1,2,3:T(2,128)(2,1)S(1)}, u32[]{:S(2)}, u32[]{:S(2)}) async-start(bf16[256,2,1,128]{0,1,2,3:T(2,128)(2,1)} %copy.45), calls=%async_computation.3 | async-start | bytes 262144 | tf_op jit(solution)/shard_map/all_to_all | solution.py:93
  242.0 22.3 %all-to-all-start.1 = ((bf16[256,2,1,128]{0,1,2,3:T(2,128)(2,1)}), bf16[256,2,1,128]{0,1,2,3:T(2,128)(2,1)S(1)}, u32[]{:S(2)}, u32[]{:S(2)}) async-start(bf16[256,2,1,128]{0,1,2,3:T(2,128)(2,1)} %copy.39), calls=%async_computation.1 | async-start | bytes 262144 | tf_op jit(solution)/shard_map/all_to_all | solution.py:61
  248.8 65.2 %all-reduce.17.cloned.1.call-start = ((), (), s32[]{:S(2)}) async-start(), calls=%async_computation.8 | async-start | bytes 409600 | tf_op jit(solution)/shard_map/psum | solution.py:99
  264.5 243.2 %copy-start.4 = (bf16[256,256]{1,0:T(8,128)(2,1)S(1)}, bf16[256,256]{1,0:T(8,128)(2,1)}, u32[]{:S(2)}) copy-start(bf16[256,256]{1,0:T(8,128)(2,1)} %param.6) | copy-start | bytes 393220
  265.8 178.0 %all-reduce.11.cloned.1.call-start = ((), (), s32[]{:S(2)}) async-start(), calls=%async_computation.5 | async-start | bytes 524288 | tf_op jit(solution)/shard_map/psum | solution.py:112
  317.3 190.1 %all-reduce.13.cloned.1.call-start = ((), (), s32[]{:S(2)}) async-start(), calls=%async_computation.6 | async-start | bytes 524288 | tf_op jit(solution)/shard_map/psum | solution.py:112
  443.9 113.8 %all-reduce.15.cloned.1.call-start = ((), (), s32[]{:S(2)}) async-start(), calls=%async_computation.7 | async-start | bytes 524288 | tf_op jit(solution)/shard_map/psum | solution.py:112
Sparse Core Ops, SparseCore 0:
  11.5 61.8 all-reduce.8
  154.7 52.2 all-reduce.18
  265.9 48.0 all-reduce.16
  317.4 126.3 all-reduce.10
  446.0 61.3 all-reduce.12
  510.2 47.4 all-reduce.14
where the time goes:
time: 567 us; the launch traced here: 566 us
  waiting for transfers between devices  453 us (80%)
  starting transfers between devices  46.9 us (8%)
  blocking collectives  21.4 us (4%)
  between operations  14.5 us (3%)
  matrix products  14.1 us (2%)
  local copies, waits for them, and re-layouts  8.99 us (2%)
  other arithmetic  7.34 us (1%)
    psum x3, waiting for transfers between devices, local(): grad_params = lax.psum(lax.psum(lax.psum(params_part, 'z'), 'y'), 'x_lo')  238 us
    psum x1, waiting for transfers between devices, local(): logits = lax.psum(partial_logits, HALF)  64.2 us
    psum x1, waiting for transfers between devices, local(): lax.psum(jnp.einsum('kf,sirk->fsir', down_slice, hidden, preferred_elemen...  52.4 us
    psum x1, waiting for transfers between devices, local(): lax.psum(dispatch_part.astype(jnp.bfloat16), HALF).astype(jnp.float32)  48.2 us
    all_to_all x1, starting transfers between devices, local(): lax.all_to_all(grad_slot_in.astype(jnp.bfloat16), EXPERT, split_axis=3, c...  16.6 us
    all_to_all x1, starting transfers between devices, local(): lax.all_to_all(slot_in, EXPERT, split_axis=3, concat_axis=3, tiled=True)  16.6 us
    all_to_all x1, waiting for transfers between devices, local(): lax.all_to_all(slot_in, EXPERT, split_axis=3, concat_axis=3, tiled=True)  15.3 us
    all_to_all x1, waiting for transfers between devices, local(): lax.all_to_all(grad_slot_in.astype(jnp.bfloat16), EXPERT, split_axis=3, c...  15 us
  transfers between devices with their start and end apart: 10, of which 10 were waited for; matrix products, arithmetic and copies ran while one was open for 1% of the time, Pallas kernels for 0%

commit v1 on v0

--- a/solution.py
+++ b/solution.py
@@ -50,10 +50,13 @@
     hidden = jax.nn.gelu(preact).astype(jnp.bfloat16)
     down_slice = down_matrix
     summed = lax.psum(
-        jnp.einsum("kf,sirk->fsir", down_slice, hidden, preferred_element_type=jnp.float32).astype(
-            jnp.bfloat16
+        lax.psum(
+            jnp.einsum(
+                "kf,sirk->fsir", down_slice, hidden, preferred_element_type=jnp.float32
+            ).astype(jnp.bfloat16),
+            "core",
         ),
-        HALF,
+        "x_hi",
     ).astype(jnp.float32)
     slot_out = lax.dynamic_slice_in_dim(
         summed, lax.axis_index(HALF) * feat_quarter, feat_quarter, 0

time: 567 us -> 635 us (1.12)
  waiting for transfers between devices: 453 us -> 512 us
  starting transfers between devices: 46.9 us -> 56.9 us
    psum x0 -> x2, waiting for transfers between devices: none -> 97.7 us  [the longest x1 61.2 us: local(): lax.psum(jnp.einsum('fk,sirk->fsir', up_slice, grad_preact, preferred_ele...]
    psum x1, waiting for transfers between devices: 52.4 us -> 27.7 us  [local(): lax.psum(jnp.einsum('kf,sirk->fsir', down_slice, hidden, preferred_elemen...]
    all_to_all x1, waiting for transfers between devices: 15 us -> 0.01 us  [local(): lax.all_to_all(grad_slot_in.astype(jnp.bfloat16), EXPERT, split_axis=3, c...]
    all_to_all x1, starting transfers between devices: 6.81 us -> 16.8 us  [local(): lax.all_to_all(slot_out.astype(jnp.bfloat16), EXPERT, split_axis=3, conca...]
  transfers between devices with their start and end apart: 10 -> 12, of which waited for: 10 -> 11; matrix products, arithmetic and copies ran while one was open for 1% -> 2% of each run, Pallas kernels for 0% -> 0%
where the time goes in v1:
time: 635 us
  waiting for transfers between devices  512 us (81%)
  starting transfers between devices  56.9 us (9%)
  blocking collectives  21.4 us (3%)
  between operations  14.4 us (2%)
  matrix products  14.2 us (2%)
  local copies, waits for them, and re-layouts  8.94 us (1%)
  other arithmetic  7.32 us (1%)
    psum x3, waiting for transfers between devices, local(): grad_params = lax.psum(lax.psum(lax.psum(params_part, 'z'), 'y'), 'x_lo')  239 us
    psum x1, waiting for transfers between devices, local(): logits = lax.psum(partial_logits, HALF)  64.2 us
    psum x1, waiting for transfers between devices, local(): lax.psum(jnp.einsum('fk,sirk->fsir', up_slice, grad_preact, preferred_ele...  61.2 us
    psum x1, waiting for transfers between devices, local(): lax.psum(dispatch_part.astype(jnp.bfloat16), HALF).astype(jnp.float32)  48 us
    psum x1, waiting for transfers between devices, local(): lax.psum(lax.psum(jnp.einsum('kf,sirk->fsir', down_slice, hidden, preferr...  36.5 us
    psum x1, waiting for transfers between devices, local(): lax.psum(jnp.einsum('kf,sirk->fsir', down_slice, hidden, preferred_elemen...  27.7 us
    all_to_all x1, starting transfers between devices, local(): lax.all_to_all(slot_out.astype(jnp.bfloat16), EXPERT, split_axis=3, conca...  16.8 us
    all_to_all x1, starting transfers between devices, local(): lax.all_to_all(slot_in, EXPERT, split_axis=3, concat_axis=3, tiled=True)  16.6 us
  transfers between devices with their start and end apart: 12, of which 11 were waited for; matrix products, arithmetic and copies ran while one was open for 2% of the time, Pallas kernels for 0%

profile of v1, /device:TPU:1, one launch (start us, length us, event | category | flops | bytes accessed | tf_op | source)
XLA Modules:
  0.0 634.7 jit_solution(14809448727358292391)
XLA Ops:
  7.2 2.0 convolution_bitcast_fusion.3
  9.2 64.2 %all-reduce.10.cloned.1.call-done = f32[1,196,256]{2,1,0:T(8,128)} async-done(((f32[1,196,256]{2,1,0:T(8,128)}), f32[1,196,256]{2,1,0:T(8,128)}) %all-reduce.10.cloned.1.call-update) | async-done | bytes 200720 | tf_op jit(solution)/shard_map/psum | solution.py:34
  73.4 1.0 fusion.82
  74.5 1.1 fusion.60
  75.6 1.1 fusion.80
  78.0 16.6 %all-to-all-start = ((bf16[2,1,256,128]{2,0,1,3:T(2,128)(2,1)}), bf16[2,1,256,128]{2,0,1,3:T(2,128)(2,1)S(1)}, u32[]{:S(2)}, u32[]{:S(2)}) async-start(bf16[2,1,256,128]{2,0,1,3:T(2,128)(2,1)} %copy.37), calls=%async_computation | async-start | bytes 262144 | tf_op jit(solution)/shard_map/all_to_all | solution.py:42
  96.0 15.3 %all-to-all-done = bf16[2,1,256,128]{2,0,1,3:T(2,128)(2,1)S(1)} async-done(((bf16[2,1,256,128]{2,0,1,3:T(2,128)(2,1)}), bf16[2,1,256,128]{2,0,1,3:T(2,128)(2,1)S(1)}, u32[]{:S(2)}, u32[]{:S(2)}) %all-to-all-start) | async-done | bytes 131104 | tf_op jit(solution)/shard_map/all_to_all | solution.py:42
  111.3 6.6 %all-to-all-start.2 = ((bf16[2,1,256,128]{2,0,1,3:T(2,128)(2,1)}), bf16[2,1,256,128]{2,0,1,3:T(2,128)(2,1)S(1)}, u32[]{:S(2)}, u32[]{:S(2)}) async-start(bf16[2,1,256,128]{2,0,1,3:T(2,128)(2,1)} %copy.43), calls=%async_computation.2 | async-start | bytes 262144 | tf_op jit(solution)/shard_map/all_to_all | solution.py:77
  118.1 10.0 %all_gather.6 = bf16[2,1,1024,128]{2,3,0,1:T(8,128)(2,1)S(1)} all-gather(bf16[2,1,256,128]{2,3,0,1:T(8,128)(2,1)S(1)} %copy.38), channel_id=1, replica_groups=mesh['y'=4,'x_lo'=2,'z'=16,'x_hi'=2,'core'=2] {'x_hi','core'}, dimensions={2}, use_global_device_ids=true | all-gather | bytes 655360 | tf_op jit(solution)/shard_map/all_gather | solution.py:46
  128.1 5.5 all-to-all-done.2
  133.5 11.5 %all_gather.7 = bf16[2,1,1024,128]{2,3,0,1:T(8,128)(2,1)S(1)} all-gather(bf16[2,1,256,128]{2,3,0,1:T(8,128)(2,1)S(1)} %copy.44), channel_id=1, replica_groups=mesh['y'=4,'x_lo'=2,'z'=16,'x_hi'=2,'core'=2] {'x_hi','core'}, dimensions={2}, use_global_device_ids=true | all-gather | bytes 655360 | tf_op jit(solution)/shard_map/all_gather | solution.py:81
  145.0 2.3 fusion.6
  147.3 1.0 copy-done.3
  148.3 1.6 fusion.14
  150.0 4.5 fusion.17
  154.6 27.7 %all-reduce.12.cloned.1.call-done = bf16[1024,2,1,128]{0,3,1,2:T(8,128)(2,1)} async-done(((bf16[1024,2,1,128]{0,3,1,2:T(8,128)(2,1)}), bf16[1024,2,1,128]{0,3,1,2:T(8,128)(2,1)}) %all-reduce.12.cloned.1.call-update) | async-done | bytes 524304 | tf_op jit(solution)/shard_map/psum | solution.py:53
  182.3 61.2 %all-reduce.16.cloned.1.call-done = bf16[1024,2,1,128]{0,3,1,2:T(8,128)(2,1)} async-done(((bf16[1024,2,1,128]{0,3,1,2:T(8,128)(2,1)}), bf16[1024,2,1,128]{0,3,1,2:T(8,128)(2,1)}) %all-reduce.16.cloned.1.call-update) | async-done | bytes 524304 | tf_op jit(solution)/shard_map/psum | solution.py:87
  243.6 0.9 convert_convert_fusion
  245.3 16.6 %all-to-all-start.3 = ((bf16[256,2,1,128]{0,1,2,3:T(2,128)(2,1)}), bf16[256,2,1,128]{0,1,2,3:T(2,128)(2,1)S(1)}, u32[]{:S(2)}, u32[]{:S(2)}) async-start(bf16[256,2,1,128]{0,1,2,3:T(2,128)(2,1)} %copy.45), calls=%async_computation.3 | async-start | bytes 262144 | tf_op jit(solution)/shard_map/all_to_all | solution.py:96
  261.9 36.5 %all-reduce.14.cloned.1.call-done = bf16[1024,2,1,128]{0,3,1,2:T(8,128)(2,1)} async-done(((bf16[1024,2,1,128]{0,3,1,2:T(8,128)(2,1)}), bf16[1024,2,1,128]{0,3,1,2:T(8,128)(2,1)}) %all-reduce.14.cloned.1.call-update) | async-done | bytes 524304 | tf_op jit(solution)/shard_map/psum | solution.py:52
  298.4 0.9 convert_convert_fusion.1
  300.1 16.8 %all-to-all-start.1 = ((bf16[256,2,1,128]{0,1,2,3:T(2,128)(2,1)}), bf16[256,2,1,128]{0,1,2,3:T(2,128)(2,1)S(1)}, u32[]{:S(2)}, u32[]{:S(2)}) async-start(bf16[256,2,1,128]{0,1,2,3:T(2,128)(2,1)} %copy.39), calls=%async_computation.1 | async-start | bytes 262144 | tf_op jit(solution)/shard_map/all_to_all | solution.py:64
  318.3 14.4 %all-to-all-done.1 = bf16[256,2,1,128]{0,1,2,3:T(2,128)(2,1)S(1)} async-done(((bf16[256,2,1,128]{0,1,2,3:T(2,128)(2,1)}), bf16[256,2,1,128]{0,1,2,3:T(2,128)(2,1)S(1)}, u32[]{:S(2)}, u32[]{:S(2)}) %all-to-all-start.1) | async-done | bytes 131104 | tf_op jit(solution)/shard_map/all_to_all | solution.py:64
  334.2 48.0 %all-reduce.24.cloned.1.call-done = (bf16[1,196,256]{2,1,0:T(8,128)(2,1)}, bf16[1,196,256]{2,1,0:T(8,128)(2,1)}) async-done(((bf16[1,196,256]{2,1,0:T(8,128)(2,1)}, bf16[1,196,256]{2,1,0:T(8,128)(2,1)}), (bf16[1,196,256]{2,1,0:T(8,128)(2,1)}, bf16[1,196,256]{2,1,0:T(8,128)(2,1)})) %all-reduce.24.cloned.1.call-update) | async-done | bytes 200720 | tf_op jit(solution)/shard_map/psum | solution.py:102
  382.2 1.2 fusion.51
  383.4 1.1 fusion.65
  384.5 0.9 convolution_bitcast_fusion
  385.5 126.5 %all-reduce.18.cloned.1.call-done = f32[256,256]{0,1:T(8,128)} async-done(((f32[256,256]{0,1:T(8,128)}), f32[256,256]{0,1:T(8,128)}) %all-reduce.18.cloned.1.call-update) | async-done | bytes 262160 | tf_op jit(solution)/shard_map/psum | solution.py:115
  512.3 63.5 %all-reduce.20.cloned.1.call-done = f32[256,256]{0,1:T(8,128)} async-done(((f32[256,256]{0,1:T(8,128)}), f32[256,256]{0,1:T(8,128)}) %all-reduce.20.cloned.1.call-update) | async-done | bytes 262160 | tf_op jit(solution)/shard_map/psum | solution.py:115
  575.8 0.9 fusion.20
  577.5 48.6 %all-reduce.22.cloned.1.call-done = f32[256,256]{0,1:T(8,128)} async-done(((f32[256,256]{0,1:T(8,128)}), f32[256,256]{0,1:T(8,128)}) %all-reduce.22.cloned.1.call-update) | async-done | bytes 262160 | tf_op jit(solution)/shard_map/psum | solution.py:115
  626.1 1.8 copy.52
  (56 shorter events, 8.6 us)
Async XLA Ops:
  7.2 141.1 %copy-start = (bf16[1,1024,1024]{2,1,0:T(8,128)(2,1)S(1)}, bf16[1,1024,1024]{2,1,0:T(8,128)(2,1)}, u32[]{:S(2)}) copy-start(bf16[1,1024,1024]{2,1,0:T(8,128)(2,1)} %param.8) | copy-start | bytes 6291460
  7.2 69.8 %copy-start.2 = (bf16[196,256]{1,0:T(8,128)(2,1)S(1)}, bf16[196,256]{1,0:T(8,128)(2,1)}, u32[]{:S(2)}) copy-start(bf16[196,256]{1,0:T(8,128)(2,1)} %param.5) | copy-start | bytes 301060
  7.2 87.8 %copy-start.5 = (bf16[196,256]{1,0:T(8,128)(2,1)S(1)}, bf16[196,256]{1,0:T(8,128)(2,1)}, u32[]{:S(2)}) copy-start(bf16[196,256]{1,0:T(8,128)(2,1)} %param.9) | copy-start | bytes 301060
  7.2 66.2 %all-reduce.10.cloned.1.call-start = ((), (), s32[]{:S(2)}) async-start(), calls=%async_computation.4 | async-start | bytes 409600 | tf_op jit(solution)/shard_map/psum | solution.py:34
  78.0 33.3 %all-to-all-start = ((bf16[2,1,256,128]{2,0,1,3:T(2,128)(2,1)}), bf16[2,1,256,128]{2,0,1,3:T(2,128)(2,1)S(1)}, u32[]{:S(2)}, u32[]{:S(2)}) async-start(bf16[2,1,256,128]{2,0,1,3:T(2,128)(2,1)} %copy.37), calls=%async_computation | async-start | bytes 262144 | tf_op jit(solution)/shard_map/all_to_all | solution.py:42
  111.3 22.2 %all-to-all-start.2 = ((bf16[2,1,256,128]{2,0,1,3:T(2,128)(2,1)}), bf16[2,1,256,128]{2,0,1,3:T(2,128)(2,1)S(1)}, u32[]{:S(2)}, u32[]{:S(2)}) async-start(bf16[2,1,256,128]{2,0,1,3:T(2,128)(2,1)} %copy.43), calls=%async_computation.2 | async-start | bytes 262144 | tf_op jit(solution)/shard_map/all_to_all | solution.py:77
  118.0 64.3 %all-reduce.12.cloned.1.call-start = ((), (), s32[]{:S(2)}) async-start(), calls=%async_computation.5 | async-start | bytes 1048576 | tf_op jit(solution)/shard_map/psum | solution.py:53
  147.3 1.0 copy-start.3
  150.0 93.6 %all-reduce.16.cloned.1.call-start = ((), (), s32[]{:S(2)}) async-start(), calls=%async_computation.7 | async-start | bytes 1048576 | tf_op jit(solution)/shard_map/psum | solution.py:87
  154.5 178.3 %copy-start.6 = (bf16[196,256]{1,0:T(8,128)(2,1)S(1)}, bf16[196,256]{1,0:T(8,128)(2,1)}, u32[]{:S(2)}) copy-start(bf16[196,256]{1,0:T(8,128)(2,1)} %param.9) | copy-start | bytes 301060
  154.6 143.8 %all-reduce.14.cloned.1.call-start = ((), (), s32[]{:S(2)}) async-start(), calls=%async_computation.6 | async-start | bytes 1048576 | tf_op jit(solution)/shard_map/psum | solution.py:52
  244.5 137.7 %copy-start.1 = (f32[1,196,256]{2,1,0:T(8,128)S(1)}, f32[1,196,256]{2,1,0:T(8,128)}, u32[]{:S(2)}) copy-start(f32[1,196,256]{2,1,0:T(8,128)} %all-reduce.10.cloned.1.call-done) | copy-start | bytes 602116
  245.3 54.8 %all-to-all-start.3 = ((bf16[256,2,1,128]{0,1,2,3:T(2,128)(2,1)}), bf16[256,2,1,128]{0,1,2,3:T(2,128)(2,1)S(1)}, u32[]{:S(2)}, u32[]{:S(2)}) async-start(bf16[256,2,1,128]{0,1,2,3:T(2,128)(2,1)} %copy.45), calls=%async_computation.3 | async-start | bytes 262144 | tf_op jit(solution)/shard_map/all_to_all | solution.py:96
  300.1 32.6 %all-to-all-start.1 = ((bf16[256,2,1,128]{0,1,2,3:T(2,128)(2,1)}), bf16[256,2,1,128]{0,1,2,3:T(2,128)(2,1)S(1)}, u32[]{:S(2)}, u32[]{:S(2)}) async-start(bf16[256,2,1,128]{0,1,2,3:T(2,128)(2,1)} %copy.39), calls=%async_computation.1 | async-start | bytes 262144 | tf_op jit(solution)/shard_map/all_to_all | solution.py:64
  316.9 65.3 %all-reduce.24.cloned.1.call-start = ((), (), s32[]{:S(2)}) async-start(), calls=%async_computation.11 | async-start | bytes 409600 | tf_op jit(solution)/shard_map/psum | solution.py:102
  332.9 243.8 %copy-start.4 = (bf16[256,256]{1,0:T(8,128)(2,1)S(1)}, bf16[256,256]{1,0:T(8,128)(2,1)}, u32[]{:S(2)}) copy-start(bf16[256,256]{1,0:T(8,128)(2,1)} %param.6) | copy-start | bytes 393220
  334.2 177.8 %all-reduce.18.cloned.1.call-start = ((), (), s32[]{:S(2)}) async-start(), calls=%async_computation.8 | async-start | bytes 524288 | tf_op jit(solution)/shard_map/psum | solution.py:115
  385.5 190.3 %all-reduce.20.cloned.1.call-start = ((), (), s32[]{:S(2)}) async-start(), calls=%async_computation.9 | async-start | bytes 524288 | tf_op jit(solution)/shard_map/psum | solution.py:115
  512.0 114.1 %all-reduce.22.cloned.1.call-start = ((), (), s32[]{:S(2)}) async-start(), calls=%async_computation.10 | async-start | bytes 524288 | tf_op jit(solution)/shard_map/psum | solution.py:115
Sparse Core Ops, SparseCore 0:
  11.5 61.8 all-reduce.9
  150.1 32.1 all-reduce.11
  185.3 58.2 all-reduce.15
  246.3 52.0 all-reduce.13
  334.3 47.8 all-reduce.23
  385.6 126.3 all-reduce.17
  514.3 61.3 all-reduce.19
  578.6 47.4 all-reduce.21
